TPU v7x, 128 devices: a whole 4x4x4 slice. The times are simulated.
128 devices in a mesh: blk: 32 (over x, y, core), mp: 4 (over z).
Axes of the slice: x: 4, y: 4, z: 4, core: 2. Of those that a mesh axis runs over, the one named last changes fastest.
Arguments:
- hidden: bfloat16 [144, 3584], replicated, may hold values from -6 to 6
- medusa_w: bfloat16 [2, 3584, 3584], P(None, 'blk', 'mp'), may hold values from -0.09375 to 0.09375
- embedding: bfloat16 [131072, 3584], P(('blk', 'mp')), may hold values from -0.5 to 0.5
- cand_ids: int32 [2, 144, 10], replicated, may hold values from 0 to 131071
- tree_q: bfloat16 [12, 48, 4096], P(None, None, 'mp'), may hold values from -6 to 6
- tree_key_value: bfloat16 [2, 12, 48, 2048], P(None, None, None, 'mp'), may hold values from -6 to 6
- prompt_key_value: bfloat16 [2, 32, 2048, 2048], P(None, 'blk', None, 'mp'), may hold values from -6 to 6
- block_group: int32 [32], P('blk'), may hold values from 0 to 11, as said below
- block_len: int32 [32], P('blk'), may hold values from 1 to 2048
- block_empty: int32 [32], P('blk'), may hold values 0 or 1
- parents: int32 [12, 48], replicated, may hold values from 0 to 46, as said below
- out_weight: bfloat16 [4096, 3584], P('mp'), may hold values from -0.09375 to 0.09375
- post_gain: float32 [3584], replicated, may hold values from 0.5 to 1.5
- resid: bfloat16 [576, 3584], P('blk'), may hold values from -6 to 6
Outputs:
- draft_logprob: float32 [2, 144, 10], replicated
- layer_out: bfloat16 [576, 3584], P('blk')
Inputs may be any that keep to these rules, and one draw needn't show every extreme that they name: `block_group`: every group number from 0 to min(12, 32) - 1 owns at least one block. `parents`: entry 0 of each row is 0; entry i for i >= 1 is below i; some group's last token has parent 48 - 2.
All inputs are finite; a program needn't handle non-finite values. No bound on the sum of `block_empty` on one device may be relied on, other than what follows from the above.
Results may differ from a plain program's by a relative error of at most 0.005.
Values may be sent and summed in bfloat16 or wider, within the bound.
A program may use at most 128 MiB of HBM per device.

v0:
```python
import jax
import jax.numpy as jnp
from jax import lax
from jax.sharding import PartitionSpec as P

HEAD_SIZE = 256


def capped(values, limit):
    return limit * jnp.tanh(values / limit)


def ancestry(parents):
    count = parents.shape[1]
    column = jnp.arange(count, dtype=jnp.int32)
    linked = (parents[:, :, None] == column[None, None, :]) & (column[None, :, None] > 0)
    reach = jnp.eye(count, dtype=jnp.float32)[None] + linked.astype(jnp.float32)
    for sweep in range(count.bit_length()):
        reach = jnp.minimum(
            jnp.einsum("gij,gjk->gik", reach, reach, precision=lax.Precision.HIGHEST), 1.0
        )
    return reach


def attend(queries, keys, values, mask):
    rows = queries.shape[0]
    length = keys.shape[0]
    kv_heads = keys.shape[1] // HEAD_SIZE
    repeats = queries.shape[1] // keys.shape[1]
    query_view = queries.reshape(rows, kv_heads, repeats, HEAD_SIZE)
    key_view = keys.reshape(length, kv_heads, HEAD_SIZE)
    value_view = values.reshape(length, kv_heads, HEAD_SIZE)
    scores = jnp.einsum(
        "qhrd,khd->hrqk", query_view, key_view, preferred_element_type=jnp.float32
    ) * HEAD_SIZE ** (-0.5)
    weights = jnp.exp(capped(scores, 50.0)) * mask[None, None]
    denominator = jnp.sum(weights, -1).transpose(2, 0, 1).reshape(rows, kv_heads * repeats)
    numerator = jnp.einsum(
        "hrqk,khd->qhrd",
        weights.astype(jnp.bfloat16),
        value_view,
        preferred_element_type=jnp.float32,
    )
    return (numerator.reshape(rows, kv_heads * repeats * HEAD_SIZE), denominator)


def per_device(
    hidden,
    medusa_w,
    embedding,
    cand_ids,
    tree_q,
    tree_key_value,
    prompt_key_value,
    block_group,
    block_len,
    block_empty,
    parents,
    out_weight,
    post_gain,
    resid,
):
    units = medusa_w.shape[2]
    inner = jnp.einsum(
        "rd,mdu->mru",
        hidden,
        lax.all_gather(medusa_w, "blk", axis=1, tiled=True),
        preferred_element_type=jnp.float32,
    )
    own_cols = lax.dynamic_slice_in_dim(hidden, lax.axis_index("mp") * units, units, 1).astype(
        jnp.float32
    )
    fresh = (own_cols[None] + jax.nn.silu(inner)).astype(jnp.bfloat16)
    full_fresh = lax.all_gather(fresh, "mp", axis=2, tiled=True)
    logits = capped(
        jnp.einsum("mrd,vd->mrv", full_fresh, embedding, preferred_element_type=jnp.float32), 30.0
    )
    totals = jnp.sum(jnp.exp(logits), -1)
    vocab_dev = embedding.shape[0]
    first_id = lax.axis_index(("blk", "mp")) * vocab_dev
    local_ids = cand_ids - first_id
    match = local_ids[..., None] == jnp.arange(vocab_dev, dtype=jnp.int32)
    picked = jnp.sum(jnp.where(match, logits[:, :, None, :], 0.0), -1)
    totals, picked = lax.psum((totals, picked), ("blk", "mp"))
    draft_logprob = picked - jnp.log(totals)[..., None]
    groups, tree_size, features = tree_q.shape
    keys = prompt_key_value[0, 0]
    values = prompt_key_value[1, 0]
    length = keys.shape[0]
    group = block_group[0]
    key_ok = ((jnp.arange(length, dtype=jnp.int32) < block_len[0]) & (block_empty[0] == 0)).astype(
        jnp.float32
    )
    row_group = jnp.arange(groups * tree_size, dtype=jnp.int32) // tree_size
    mask = (row_group == group).astype(jnp.float32)[:, None] * key_ok[None, :]
    numer, denom = attend(tree_q.reshape(groups * tree_size, features), keys, values, mask)
    rows_dev = groups * tree_size // lax.axis_size("blk")
    first_row = lax.axis_index("blk") * rows_dev
    summed = lax.psum((numer, denom), "blk")
    numer = lax.dynamic_slice_in_dim(summed[0], first_row, rows_dev, 0)
    denom = lax.dynamic_slice_in_dim(summed[1], first_row, rows_dev, 0)
    reach = ancestry(parents)
    tree_numer, tree_denom = jax.vmap(attend)(tree_q, tree_key_value[0], tree_key_value[1], reach)
    heads_dev = tree_denom.shape[2]
    tree_numer = lax.dynamic_slice_in_dim(
        tree_numer.reshape(groups * tree_size, features), first_row, rows_dev, 0
    )
    tree_denom = lax.dynamic_slice_in_dim(
        tree_denom.reshape(groups * tree_size, heads_dev), first_row, rows_dev, 0
    )
    numer = numer + tree_numer
    denom = denom + tree_denom
    heads_out = (
        (numer.reshape(rows_dev, heads_dev, HEAD_SIZE) / denom[..., None])
        .reshape(rows_dev, features)
        .astype(jnp.bfloat16)
    )
    attn = lax.psum(jnp.dot(heads_out, out_weight, preferred_element_type=jnp.float32), "mp")
    normed = attn * lax.rsqrt(jnp.mean(attn * attn, -1, keepdims=True) + 1e-06) * post_gain
    layer_out = (normed + resid.astype(jnp.float32)).astype(jnp.bfloat16)
    return (draft_logprob, layer_out)


def solution(mesh):
    placed = (
        P(),
        P(None, "blk", "mp"),
        P(("blk", "mp"), None),
        P(),
        P(None, None, "mp"),
        P(None, None, None, "mp"),
        P(None, "blk", None, "mp"),
        P("blk"),
        P("blk"),
        P("blk"),
        P(),
        P("mp", None),
        P(),
        P("blk", None),
    )
    return jax.shard_map(
        per_device, mesh=mesh, in_specs=placed, out_specs=(P(), P("blk", None)), check_vma=False
    )
```

profile of v0, /device:TPU:1, one launch (start us, length us, event | category | flops | bytes accessed | tf_op | source)
XLA Modules:
  0.0 381.7 jit_solution(4261685247920140671)
XLA Ops:
  7.2 0.0 all-reduce.4.cloned.1.call-start
  7.2 4.4 %fusion.51 = (bf16[1,1,2048,512]{3,2,1,0:T(8,128)(2,1)}, bf16[1,1,2048,512]{3,2,1,0:T(8,128)(2,1)}) fusion(bf16[2,1,2048,512]{3,2,1,0:T(8,128)(2,1)} %param.20), kind=kLoop, calls=%fused_computation.70 | loop fusion | bytes 8388608 | tf_op jit(solution)/shard_map/slice | solution.py:88
  11.6 2.9 copy.79
  16.5 3.3 reshape_reshape.3
  19.8 4.0 %copy.80 = bf16[1,1,2048,512]{2,3,1,0:T(8,128)(2,1)} copy(bf16[1,1,2048,512]{3,2,1,0:T(8,128)(2,1)} %get-tuple-element.6) | data formatting | bytes 4194304
  23.8 0.4 broadcast_multiply_fusion
  24.2 10.5 %fusion = (f32[2,2,576]{2,1,0:T(2,128)}, f32[2,2048,576,2]{1,2,3,0:T(8,128)}) fusion(f32[576,2048]{1,0:T(8,128)S(1)} %broadcast_multiply_fusion, bf16[2048,2,256,1]{0,2,3,1:T(8,128)(2,1)S(1)} %bitcast.83, bf16[576,2,2,256]{3,2,1,0:T(2,128)(2,1)S(1)} %reshape_reshape.3), kind=kOutput, calls=%fused_computation.1 | convolution fusion | flops 2434791168 | bytes 26878976 | tf_op jit(solution)/shard_map/qhrd,khd->hrqk/dot_general | solution.py:33
  34.7 9.1 %fusion.6 = f32[576,2,2,256]{3,0,2,1:T(8,128)S(1)} fusion(bf16[2048,2,256,1]{0,2,3,1:T(8,128)(2,1)S(1)} %bitcast.85, f32[2,2048,576,2]{1,2,3,0:T(8,128)} %get-tuple-element.15, f32[576,2048]{1,0:T(8,128)S(1)} %broadcast_multiply_fusion), kind=kOutput, calls=%fused_computation.10 | convolution fusion | flops 2434793472 | bytes 28049408 | tf_op jit(solution)/shard_map/hrqk,khd->qhrd/dot_general | solution.py:38
  43.8 1.8 copy.56
  45.6 2.9 reshape.101
  48.6 0.0 all-gather.3.cloned.1.call-start
  48.6 0.7 all-gather.3.cloned.1.call-update
  49.3 0.2 all-reduce.6.cloned.1.call-start
  49.6 0.3 copy-done
  49.8 0.9 reshape.102
  50.7 0.7 reshape.104
  51.4 0.1 fusion.52
  51.5 0.1 reshape_squeeze.14
  51.7 1.4 convolution_minimum_fusion.5
  53.1 0.4 convolution_minimum_fusion.4
  53.5 0.4 convolution_minimum_fusion.3
  53.9 0.4 convolution_minimum_fusion.2
  54.4 0.4 convolution_minimum_fusion.1
  54.8 0.4 convolution_minimum_fusion
  55.2 0.1 copy.59
  55.3 0.9 fusion.53
  56.2 0.1 reshape.105
  56.3 124.9 %psum.38 = f32[576,4]{0,1:T(4,128)S(1)} all-reduce(f32[576,4]{0,1:T(4,128)S(1)} %reshape.104), channel_id=1, replica_groups=mesh['blk'=32,'mp'=4] {'blk'}, use_global_device_ids=true, to_apply=%region_6.7 | all-reduce | flops 2304 | bytes 18432 | tf_op jit(solution)/shard_map/psum | solution.py:99
  181.2 0.1 dynamic-slice_add_fusion
  181.3 0.1 copy.64
  181.4 0.1 div.48
  181.5 0.1 reshape_squeeze.15
  181.7 0.5 convolution_bitcast_fusion
  182.2 1.8 copy.62
  184.1 2.9 reshape.103
  187.0 0.0 all-reduce.4.cloned.1.call-done
  187.1 5.1 %fusion.39 = f32[18,3584]{1,0:T(8,128)} fusion(bf16[1024,3584]{1,0:T(8,128)(2,1)} %param.25, f32[18,1024]{1,0:T(8,128)S(1)} %bitcast.87, f32[576,1024]{1,0:T(8,128)} %reshape.103, s32[]{:T(128)S(6)} %select_n.25, f32[576,1024]{1,0:T(8,128)} %all-reduce.4.cloned.1.call-done), kind=kOutput, calls=%fused_computation.47 | convolution fusion | flops 132175872 | bytes 7868420 | tf_op jit(solution)/shard_map/dot_general | solution.py:118
  192.2 0.3 all-gather.5.cloned.1.call-start
  192.4 32.7 %all-gather.3.cloned.1.call-done = bf16[2,3584,896]{2,1,0:T(8,128)(2,1)} async-done(((bf16[2,112,896]{2,1,0:T(8,128)(2,1)}), bf16[2,3584,896]{2,1,0:T(8,128)(2,1)}) %all-gather.3.cloned.1.call-update) | async-done | bytes 12845072 | tf_op jit(solution)/shard_map/all_gather | solution.py:67
  225.2 7.6 %add_convert_fusion = bf16[2,144,896]{2,1,0:T(8,128)(2,1)} fusion(bf16[2,3584,896]{2,1,0:T(8,128)(2,1)} %all-gather.3.cloned.1.call-done, bf16[144,3584]{1,0:T(8,128)(2,1)S(1)} %copy-done.4, f32[144,896]{1,0:T(8,128)S(1)} %dynamic-slice_convert_fusion), kind=kOutput, calls=%fused_computation.32 | convolution fusion | flops 1851236352 | bytes 14909440 | tf_op jit(solution)/shard_map/rd,mdu->mru/dot_general | solution.py:64
  232.8 34.1 %all-reduce.6.cloned.1.call-done = f32[18,3584]{1,0:T(8,128)} async-done(((f32[18,3584]{1,0:T(8,128)}), f32[18,3584]{1,0:T(8,128)}) %all-reduce.6.cloned.1.call-update) | async-done | bytes 258064 | tf_op jit(solution)/shard_map/psum | solution.py:118
  266.9 1.1 multiply_reduce_fusion
  268.0 1.8 add_convert_fusion.1
  269.8 31.7 %all-gather.5.cloned.1.call-done = bf16[2,144,3584]{2,1,0:T(8,128)(2,1)} async-done(((bf16[2,144,896]{2,1,0:T(8,128)(2,1)}), bf16[2,144,3584]{2,1,0:T(8,128)(2,1)}) %all-gather.5.cloned.1.call-update) | async-done | bytes 2064400 | tf_op jit(solution)/shard_map/all_gather | solution.py:74
  301.5 6.2 %exponential_reduce_fusion = (f32[2,144]{1,0:T(2,128)S(1)}, f32[2,144,1024]{2,1,0:T(8,128)S(1)}) fusion(bf16[2,144,3584]{2,1,0:T(8,128)(2,1)} %all-gather.5.cloned.1.call-done, bf16[1024,3584]{1,0:T(8,128)(2,1)} %param.16), kind=kOutput, calls=%fused_computation.24 | convolution fusion | flops 2114813696 | bytes 10585216 | tf_op jit(solution)/shard_map/mrd,vd->mrv/dot_general | solution.py:76
  307.8 1.8 select_reduce_fusion
  309.6 64.9 %all-reduce = (f32[2,144,10]{1,2,0:T(8,128)S(1)}, f32[2,144]{1,0:T(2,128)S(1)}) all-reduce(f32[2,144,10]{1,2,0:T(8,128)S(1)} %select_reduce_fusion, f32[2,144]{1,0:T(2,128)S(1)} %get-tuple-element.10), channel_id=1, replica_groups=mesh['blk'=32,'mp'=4] {'blk','mp'}, use_global_device_ids=true, to_apply=%region_1.2 | all-reduce | flops 3168 | bytes 25344 | tf_op jit(solution)/shard_map/psum | solution.py:84
  374.5 0.6 copy.65
  (29 shorter events, 0.2 us)
Async XLA Ops:
  7.2 179.9 %all-reduce.4.cloned.1.call-start = ((), (), s32[]{:S(2)}) async-start(), calls=%async_computation.2 | async-start | bytes 4718592 | tf_op jit(solution)/shard_map/psum | solution.py:99
  24.2 10.5 %copy-start.1 = (bf16[1,1,2048,512]{2,3,1,0:T(8,128)(2,1)S(1)}, bf16[1,1,2048,512]{2,3,1,0:T(8,128)(2,1)}, u32[]{:S(2)}) copy-start(bf16[1,1,2048,512]{2,3,1,0:T(8,128)(2,1)} %copy.80) | copy-start | bytes 6291460
  48.6 1.3 copy-start
  48.6 2.9 copy-start.2
  48.6 176.6 %all-gather.3.cloned.1.call-start = ((), (), s32[]{:S(2)}) async-start(), calls=%async_computation | async-start | bytes 13246464 | tf_op jit(solution)/shard_map/all_gather | solution.py:67
  49.3 217.6 %all-reduce.6.cloned.1.call-start = ((), (), s32[]{:S(2)}) async-start(), calls=%async_computation.3 | async-start | bytes 688128 | tf_op jit(solution)/shard_map/psum | solution.py:118
  184.0 3.0 copy-start.4
  192.1 40.7 %copy-start.5 = (s32[2,144,10]{1,0,2:T(2,128)S(1)}, s32[2,144,10]{1,0,2:T(2,128)}, u32[]{:S(2)}) copy-start(s32[2,144,10]{1,0,2:T(2,128)} %param.17) | copy-start | bytes 34564
  192.2 75.9 %copy-start.3 = (bf16[18,3584]{1,0:T(8,128)(2,1)S(1)}, bf16[18,3584]{1,0:T(8,128)(2,1)}, u32[]{:S(2)}) copy-start(bf16[18,3584]{1,0:T(8,128)(2,1)} %param.27) | copy-start | bytes 387076
  192.2 75.9 %copy-start.6 = (f32[3584]{0:T(1024)S(1)}, f32[3584]{0:T(1024)}, u32[]{:S(2)}) copy-start(f32[3584]{0:T(1024)} %param.26) | copy-start | bytes 43012
  192.2 109.4 %all-gather.5.cloned.1.call-start = ((), (), s32[]{:S(2)}) async-start(), calls=%async_computation.1 | async-start | bytes 2580480 | tf_op jit(solution)/shard_map/all_gather | solution.py:74
Sparse Core Ops, SparseCore 0:
  48.7 110.4 all-reduce.3
  161.6 63.5 all-gather.2
  227.5 39.3 all-reduce.5
  268.4 33.0 all-gather.4
where the time goes:
time: 382 us
  blocking collectives  190 us (50%)
  waiting for transfers between devices  99.3 us (26%)
  matrix products  43.3 us (11%)
  local copies, waits for them, and re-layouts  27.5 us (7%)
  between operations  16 us (4%)
  other arithmetic  5.25 us (1%)
    psum x1, blocking collectives, per_device(): summed = lax.psum((numer, denom), 'blk')  125 us
    psum x1, blocking collectives, per_device(): totals, picked = lax.psum((totals, picked), ('blk', 'mp'))  64.9 us
    psum x1, waiting for transfers between devices, per_device(): lax.psum(jnp.dot(heads_out, out_weight, preferred_element_type=jnp.float3...  34.1 us
    all_gather x1, waiting for transfers between devices, per_device(): lax.all_gather(medusa_w, 'blk', axis=1, tiled=True)  32.7 us
    all_gather x1, waiting for transfers between devices, per_device(): full_fresh = lax.all_gather(fresh, 'mp', axis=2, tiled=True)  31.7 us
    dot_general x2, matrix products, attend(): jnp.einsum('qhrd,khd->hrqk', query_view, key_view, preferred_element_type...  11.3 us
    dot_general x2, matrix products, attend(): jnp.einsum('hrqk,khd->qhrd', weights.astype(jnp.bfloat16), value_view, pr...  9.63 us
    unnamed x19, local copies, waits for them, and re-layouts  7.84 us
  transfers between devices with their start and end apart: 4, of which 3 were waited for; matrix products, arithmetic and copies ran while one was open for 7% of the time, Pallas kernels for 0%

commit v1 on v0

--- a/solution.py
+++ b/solution.py
@@ -71,7 +71,22 @@
         jnp.float32
     )
     fresh = (own_cols[None] + jax.nn.silu(inner)).astype(jnp.bfloat16)
-    full_fresh = lax.all_gather(fresh, "mp", axis=2, tiled=True)
+    ways, here, step = (lax.axis_size("mp"), lax.axis_index("mp"), fresh.shape[2])
+    shape = [n * ways if d == 2 else n for d, n in enumerate(fresh.shape)]
+    full_fresh = lax.dynamic_update_slice_in_dim(
+        jnp.zeros(shape, fresh.dtype), fresh, here * step, axis=2
+    )
+    going_up = going_down = fresh
+    for far in range(1, ways // 2 + 1):
+        going_up = lax.ppermute(going_up, "mp", [(d, (d + 1) % ways) for d in range(ways)])
+        full_fresh = lax.dynamic_update_slice_in_dim(
+            full_fresh, going_up, (here - far) % ways * step, axis=2
+        )
+        if 2 * far < ways:
+            going_down = lax.ppermute(going_down, "mp", [(d, (d - 1) % ways) for d in range(ways)])
+            full_fresh = lax.dynamic_update_slice_in_dim(
+                full_fresh, going_down, (here + far) % ways * step, axis=2
+            )
     logits = capped(
         jnp.einsum("mrd,vd->mrv", full_fresh, embedding, preferred_element_type=jnp.float32), 30.0
     )

time: 382 us -> 365 us (0.955)
  waiting for transfers between devices: 99.3 us -> 76.3 us
    all_gather x1 -> x0, waiting for transfers between devices: 31.7 us -> none  [per_device(): full_fresh = lax.all_gather(fresh, 'mp', axis=2, tiled=True)]
    ppermute x0 -> x3, waiting for transfers between devices: none -> 9.6 us  [the longest x1 7.08 us: per_device(): lax.ppermute(going_down, 'mp', [(d, (d - 1) % ways) for d in range(ways)])]
    unnamed x19 -> x17, local copies, waits for them, and re-layouts: 7.84 us -> 7.78 us
  transfers between devices with their start and end apart: 4 -> 6, of which waited for: 3 -> 4; matrix products, arithmetic and copies ran while one was open for 7% -> 8% of each run, Pallas kernels for 0% -> 0%
where the time goes in v1:
time: 365 us
  blocking collectives  193 us (53%)
  waiting for transfers between devices  76.3 us (21%)
  matrix products  42.3 us (12%)
  local copies, waits for them, and re-layouts  27.7 us (8%)
  between operations  16.1 us (4%)
  other arithmetic  6.19 us (2%)
    psum x1, blocking collectives, per_device(): summed = lax.psum((numer, denom), 'blk')  125 us
    psum x1, blocking collectives, per_device(): totals, picked = lax.psum((totals, picked), ('blk', 'mp'))  68 us
    psum x1, waiting for transfers between devices, per_device(): lax.psum(jnp.dot(heads_out, out_weight, preferred_element_type=jnp.float3...  33.9 us
    all_gather x1, waiting for transfers between devices, per_device(): lax.all_gather(medusa_w, 'blk', axis=1, tiled=True)  32.1 us
    dot_general x2, matrix products, attend(): jnp.einsum('qhrd,khd->hrqk', query_view, key_view, preferred_element_type...  11.3 us
    dot_general x2, matrix products, attend(): jnp.einsum('hrqk,khd->qhrd', weights.astype(jnp.bfloat16), value_view, pr...  9.63 us
    unnamed x17, local copies, waits for them, and re-layouts  7.78 us
  transfers between devices with their start and end apart: 6, of which 4 were waited for; matrix products, arithmetic and copies ran while one was open for 8% of the time, Pallas kernels for 0%

profile of v1, /device:TPU:1, one launch (start us, length us, event | category | flops | bytes accessed | tf_op | source)
XLA Modules:
  0.0 364.7 jit_solution(16832484123569222972)
XLA Ops:
  7.2 4.4 %fusion.52 = (bf16[1,1,2048,512]{3,2,1,0:T(8,128)(2,1)}, bf16[1,1,2048,512]{3,2,1,0:T(8,128)(2,1)}) fusion(bf16[2,1,2048,512]{3,2,1,0:T(8,128)(2,1)} %param.20), kind=kLoop, calls=%fused_computation.76 | loop fusion | bytes 8388608 | tf_op jit(solution)/shard_map/slice | solution.py:103
  11.6 2.9 copy.79
  16.5 3.3 reshape_reshape.3
  19.8 4.0 %copy.80 = bf16[1,1,2048,512]{2,3,1,0:T(8,128)(2,1)} copy(bf16[1,1,2048,512]{3,2,1,0:T(8,128)(2,1)} %get-tuple-element.6) | data formatting | bytes 4194304
  23.8 0.4 broadcast_multiply_fusion
  24.2 10.5 %fusion = (f32[2,2,576]{2,1,0:T(2,128)}, f32[2,2048,576,2]{1,2,3,0:T(8,128)}) fusion(f32[576,2048]{1,0:T(8,128)S(1)} %broadcast_multiply_fusion, bf16[2048,2,256,1]{0,2,3,1:T(8,128)(2,1)S(1)} %bitcast.85, bf16[576,2,2,256]{3,2,1,0:T(2,128)(2,1)S(1)} %reshape_reshape.3), kind=kOutput, calls=%fused_computation.1 | convolution fusion | flops 2434791168 | bytes 26878976 | tf_op jit(solution)/shard_map/qhrd,khd->hrqk/dot_general | solution.py:33
  34.7 9.1 %fusion.6 = f32[576,2,2,256]{3,0,2,1:T(8,128)S(1)} fusion(bf16[2048,2,256,1]{0,2,3,1:T(8,128)(2,1)S(1)} %bitcast.87, f32[2,2048,576,2]{1,2,3,0:T(8,128)} %get-tuple-element.17, f32[576,2048]{1,0:T(8,128)S(1)} %broadcast_multiply_fusion), kind=kOutput, calls=%fused_computation.10 | convolution fusion | flops 2434793472 | bytes 28049408 | tf_op jit(solution)/shard_map/hrqk,khd->qhrd/dot_general | solution.py:38
  43.8 1.8 copy.56
  45.6 2.9 reshape.101
  48.6 0.7 all-gather.2.cloned.1.call-update
  49.3 0.2 all-reduce.6.cloned.1.call-start
  49.6 0.2 copy-done
  49.8 0.9 reshape.102
  50.7 0.7 reshape.104
  51.5 0.1 fusion.53
  51.5 0.1 reshape_squeeze.14
  51.7 1.4 convolution_minimum_fusion.5
  53.1 0.4 convolution_minimum_fusion.4
  53.5 0.4 convolution_minimum_fusion.3
  53.9 0.4 convolution_minimum_fusion.2
  54.4 0.4 convolution_minimum_fusion.1
  54.8 0.4 convolution_minimum_fusion
  55.2 0.1 copy.59
  55.3 0.9 fusion.54
  56.2 0.1 reshape.105
  56.3 124.9 %psum.38 = f32[576,4]{0,1:T(4,128)S(1)} all-reduce(f32[576,4]{0,1:T(4,128)S(1)} %reshape.104), channel_id=1, replica_groups=mesh['blk'=32,'mp'=4] {'blk'}, use_global_device_ids=true, to_apply=%region_6.7 | all-reduce | flops 2304 | bytes 18432 | tf_op jit(solution)/shard_map/psum | solution.py:114
  181.3 0.1 copy.64
  181.4 0.1 div.48
  181.5 0.1 reshape_squeeze.15
  181.7 0.5 convolution_bitcast_fusion
  182.2 1.8 copy.62
  184.0 2.9 reshape.103
  187.0 1.0 dynamic-slice_convert_fusion
  188.0 5.1 %fusion.39 = f32[18,3584]{1,0:T(8,128)} fusion(bf16[1024,3584]{1,0:T(8,128)(2,1)} %param.25, f32[18,1024]{1,0:T(8,128)S(1)} %bitcast.89, f32[576,1024]{1,0:T(8,128)} %reshape.103, s32[]{:T(128)S(6)} %select_n.56, f32[576,1024]{1,0:T(8,128)} %all-reduce.4.cloned.1.call-done), kind=kOutput, calls=%fused_computation.47 | convolution fusion | flops 132175872 | bytes 7868420 | tf_op jit(solution)/shard_map/dot_general | solution.py:133
  193.1 32.1 %all-gather.2.cloned.1.call-done = bf16[2,3584,896]{2,1,0:T(8,128)(2,1)} async-done(((bf16[2,112,896]{2,1,0:T(8,128)(2,1)}), bf16[2,3584,896]{2,1,0:T(8,128)(2,1)}) %all-gather.2.cloned.1.call-update) | async-done | bytes 12845072 | tf_op jit(solution)/shard_map/all_gather | solution.py:67
  225.2 0.1 broadcast_in_dim.14
  225.3 7.2 %constant_dynamic-update-slice_fusion.3 = (bf16[2,144,3584]{2,1,0:T(8,128)(2,1)S(1)}, bf16[2,144,896]{2,1,0:T(8,128)(2,1)S(1)}) fusion(bf16[2,144,3584]{2,1,0:T(8,128)(2,1)S(1)} %broadcast_in_dim.14, s32[]{:T(128)S(6)} %select_n.47, bf16[2,3584,896]{2,1,0:T(8,128)(2,1)} %all-gather.2.cloned.1.call-done, bf16[144,3584]{1,0:T(8,128)(2,1)} %param.14, ...), kind=kOutput, calls=%fused_computation.70 | convolution fusion | flops 1851236352 | bytes 15425540 | tf_op jit(solution)/shard_map/rd,mdu->mru/dot_general | solution.py:64
  232.5 1.3 collective-permute-start
  233.9 33.9 %all-reduce.6.cloned.1.call-done = f32[18,3584]{1,0:T(8,128)} async-done(((f32[18,3584]{1,0:T(8,128)}), f32[18,3584]{1,0:T(8,128)}) %all-reduce.6.cloned.1.call-update) | async-done | bytes 258064 | tf_op jit(solution)/shard_map/psum | solution.py:133
  267.8 1.1 multiply_reduce_fusion
  268.9 1.6 collective-permute-start.1
  270.5 1.8 add_convert_fusion.1
  272.4 7.1 %collective-permute-done.1 = bf16[2,144,896]{2,1,0:T(8,128)(2,1)S(1)} collective-permute-done((bf16[2,144,896]{2,1,0:T(8,128)(2,1)S(1)}, bf16[2,144,896]{2,1,0:T(8,128)(2,1)S(1)}, u32[]{:S(2)}, u32[]{:S(2)}) %collective-permute-start.1) | collective-permute-done | bytes 516128 | tf_op jit(solution)/shard_map/ppermute | solution.py:86
  279.5 2.5 collective-permute-done.2
  282.1 5.6 %exponential_reduce_fusion = (f32[2,144]{1,0:T(2,128)S(1)}, f32[2,144,1024]{2,1,0:T(8,128)S(1)}) fusion(bf16[2,144,3584]{2,1,0:T(8,128)(2,1)S(1)} %constant_dynamic-update-slice_fusion, bf16[1024,3584]{1,0:T(8,128)(2,1)} %param.16), kind=kOutput, calls=%fused_computation.24 | convolution fusion | flops 2114813696 | bytes 10585216 | tf_op jit(solution)/shard_map/mrd,vd->mrv/dot_general | solution.py:91
  287.7 1.8 select_reduce_fusion
  289.5 68.0 %all-reduce = (f32[2,144,10]{1,2,0:T(8,128)S(1)}, f32[2,144]{1,0:T(2,128)S(1)}) all-reduce(f32[2,144,10]{1,2,0:T(8,128)S(1)} %select_reduce_fusion, f32[2,144]{1,0:T(2,128)S(1)} %get-tuple-element.12), channel_id=1, replica_groups=mesh['blk'=32,'mp'=4] {'blk','mp'}, use_global_device_ids=true, to_apply=%region_1.2 | all-reduce | flops 3168 | bytes 25344 | tf_op jit(solution)/shard_map/psum | solution.py:99
  357.5 0.6 copy.65
  (34 shorter events, 0.5 us)
Async XLA Ops:
  7.2 180.8 %all-reduce.4.cloned.1.call-start = ((), (), s32[]{:S(2)}) async-start(), calls=%async_computation.1 | async-start | bytes 4718592 | tf_op jit(solution)/shard_map/psum | solution.py:114
  24.2 10.5 %copy-start.1 = (bf16[1,1,2048,512]{2,3,1,0:T(8,128)(2,1)S(1)}, bf16[1,1,2048,512]{2,3,1,0:T(8,128)(2,1)}, u32[]{:S(2)}) copy-start(bf16[1,1,2048,512]{2,3,1,0:T(8,128)(2,1)} %copy.80) | copy-start | bytes 6291460
  48.6 1.3 copy-start
  48.6 2.9 copy-start.2
  48.6 176.6 %all-gather.2.cloned.1.call-start = ((), (), s32[]{:S(2)}) async-start(), calls=%async_computation | async-start | bytes 13246464 | tf_op jit(solution)/shard_map/all_gather | solution.py:67
  49.3 218.5 %all-reduce.6.cloned.1.call-start = ((), (), s32[]{:S(2)}) async-start(), calls=%async_computation.2 | async-start | bytes 688128 | tf_op jit(solution)/shard_map/psum | solution.py:133
  225.3 8.6 %copy-start.4 = (s32[2,144,10]{1,0,2:T(2,128)S(1)}, s32[2,144,10]{1,0,2:T(2,128)}, u32[]{:S(2)}) copy-start(s32[2,144,10]{1,0,2:T(2,128)} %param.17) | copy-start | bytes 34564
  225.3 45.2 %copy-start.3 = (bf16[18,3584]{1,0:T(8,128)(2,1)S(1)}, bf16[18,3584]{1,0:T(8,128)(2,1)}, u32[]{:S(2)}) copy-start(bf16[18,3584]{1,0:T(8,128)(2,1)} %param.27) | copy-start | bytes 387076
  225.3 45.2 %copy-start.5 = (f32[3584]{0:T(1024)S(1)}, f32[3584]{0:T(1024)}, u32[]{:S(2)}) copy-start(f32[3584]{0:T(1024)} %param.26) | copy-start | bytes 43012
  232.5 38.0 %collective-permute-start = (bf16[2,144,896]{2,1,0:T(8,128)(2,1)S(1)}, bf16[2,144,896]{2,1,0:T(8,128)(2,1)S(1)}, u32[]{:S(2)}, u32[]{:S(2)}) collective-permute-start(bf16[2,144,896]{2,1,0:T(8,128)(2,1)S(1)} %get-tuple-element.11), channel_id=1, source_target_pairs={{0,1},{1,2},{2,3},{3,0},{4,5},{5,6},{6,7},{7,4},{8,9},{9,10},{10,1... | collective-permute-start | bytes 1548296 | tf_op jit(solution)/shard_map/ppermute | solution.py:81
  268.9 10.5 %collective-permute-start.1 = (bf16[2,144,896]{2,1,0:T(8,128)(2,1)S(1)}, bf16[2,144,896]{2,1,0:T(8,128)(2,1)S(1)}, u32[]{:S(2)}, u32[]{:S(2)}) collective-permute-start(bf16[2,144,896]{2,1,0:T(8,128)(2,1)S(1)} %get-tuple-element.11), channel_id=1, source_target_pairs={{0,3},{1,0},{2,1},{3,2},{4,7},{5,4},{6,5},{7,6},{8,11},{9,8},{10,9... | collective-permute-start | bytes 1548296 | tf_op jit(solution)/shard_map/ppermute | solution.py:86
  270.5 11.5 %collective-permute-start.2 = (bf16[2,144,896]{2,1,0:T(8,128)(2,1)S(1)}, bf16[2,144,896]{2,1,0:T(8,128)(2,1)S(1)}, u32[]{:S(2)}, u32[]{:S(2)}) collective-permute-start(bf16[2,144,896]{2,1,0:T(8,128)(2,1)S(1)} %collective-permute-done), channel_id=1, source_target_pairs={{0,1},{1,2},{2,3},{3,0},{4,5},{5,6},{6,7},{7,4},{8,9},{9,10},{10,1... | collective-permute-start | bytes 1548296 | tf_op jit(solution)/shard_map/ppermute | solution.py:81
Sparse Core Ops, SparseCore 0:
  48.7 110.4 all-reduce.3
  161.6 63.5 all-gather.1
  227.5 40.2 all-reduce.5
